TPU v7x, 256 devices: a whole 4x4x8 slice. The times are simulated.
256 devices in a mesh: dp: 8 (over y, core), ctx: 32 (over x, z).
Axes of the slice: x: 4, y: 4, z: 8, core: 2. Of those that a mesh axis runs over, the one named last changes fastest.
Arguments:
- features: bfloat16 [8, 4096, 1536], P('dp', 'ctx'), may hold values from -6 to 6
- short_weight: float32 [7, 1536], replicated, may hold values from -2 to 2
- long_filter: float32 [4096, 512], P('ctx'), may hold values from -4 to 4
- skip_bias: float32 [512], replicated, may hold values from 0.5 to 1.5
- cotangent: bfloat16 [8, 4096, 512], P('dp', 'ctx'), may hold values from -6 to 6
Outputs:
- layer_out: bfloat16 [8, 4096, 512], P('dp', 'ctx')
- grad_features: bfloat16 [8, 4096, 1536], P('dp', 'ctx')
- grad_short: float32 [7, 1536], replicated
- grad_filter: float32 [4096, 512], P('ctx')
- grad_skip: float32 [512], replicated
All inputs are finite; a program needn't handle non-finite values.
Results may differ from a plain program's by a relative error of at most 0.001.
Values may be sent and summed in bfloat16 or wider, within the bound.
A program may use at most 64 MiB of HBM per device.

v0:
```python
import math
import jax
import jax.numpy as jnp
from jax import lax
from jax.sharding import PartitionSpec as P

PRECISE = lax.Precision.HIGHEST


def swapped(value, axis, distance):
    mask = 2**distance
    pairs = [(source, source ^ mask) for source in range(lax.axis_size(axis))]
    return lax.ppermute(value, axis, pairs)


def shifted(value, axis, steps):
    count = lax.axis_size(axis)
    initial, last = (max(0, -steps), min(count, count - steps))
    return lax.ppermute(value, axis, [(source, source + steps) for source in range(initial, last)])


def bit_reverse(index_value, bit_count):
    reversed_value = jnp.zeros_like(index_value)
    for bit_place in range(bit_count):
        digit_now = index_value // 2**bit_place % 2
        reversed_value = reversed_value + digit_now * 2 ** (bit_count - 1 - bit_place)
    return reversed_value


def spectral_table(device, parts_count, tokens):
    bit_count = parts_count.bit_length() - 1
    coarse_freq = 2 * bit_reverse(device, bit_count) + jnp.arange(2, dtype=jnp.int32)
    total_points = 2 * parts_count * tokens
    column_index = jnp.arange(tokens, dtype=jnp.int32)
    full_freq = coarse_freq[:, None] + 2 * parts_count * column_index[None, :]
    phase_value = column_index[None, None, :] * full_freq[:, :, None] % total_points
    angle_value = phase_value.astype(jnp.float32) * (2.0 * math.pi / total_points)
    return (jnp.cos(angle_value), -jnp.sin(angle_value))


def contract(matrix, values):
    return jnp.einsum("akm,amw->akw", matrix, values, precision=PRECISE)


def contract_back(matrix, values):
    return jnp.einsum("akm,akw->amw", matrix, values, precision=PRECISE)


def local_forward(spec_real, spec_imag, table):
    table_real, table_imag = table
    out_real = contract(table_real, spec_real) - contract(table_imag, spec_imag)
    out_imag = contract(table_real, spec_imag) + contract(table_imag, spec_real)
    return (out_real, out_imag)


def local_inverse(spec_real, spec_imag, table):
    table_real, table_imag = table
    factor = 1.0 / spec_real.shape[1]
    out_real = (
        contract_back(table_real, spec_real) + contract_back(table_imag, spec_imag)
    ) * factor
    out_imag = (
        contract_back(table_real, spec_imag) - contract_back(table_imag, spec_real)
    ) * factor
    return (out_real, out_imag)


def pair_swap(stacked, bit_place):
    return swapped(stacked, "ctx", bit_place)


def pair_swap_back(stacked, bit_place):
    return swapped(stacked, "ctx", bit_place)


def section_terms(device, bit_place):
    span_size = 2**bit_place
    upper_flag = device // span_size % 2
    sign_value = (1 - 2 * upper_flag).astype(jnp.float32)
    turn_value = math.pi / span_size * (upper_flag * (device % span_size)).astype(jnp.float32)
    return (sign_value, jnp.cos(turn_value), jnp.sin(turn_value))


def butterfly_forward(signals):
    parts_count = lax.axis_size("ctx")
    device = lax.axis_index("ctx")
    bit_count = parts_count.bit_length() - 1
    angle_value = math.pi * device.astype(jnp.float32) / parts_count
    spec_real = jnp.stack([signals, signals * jnp.cos(angle_value)])
    spec_imag = jnp.stack([jnp.zeros_like(signals), -signals * jnp.sin(angle_value)])
    for bit_place in reversed(range(bit_count)):
        sign_value, cos_turn, sin_turn = section_terms(device, bit_place)
        partner = pair_swap(jnp.stack([spec_real, spec_imag]), bit_place)
        joined_real = partner[0] + sign_value * spec_real
        joined_imag = partner[1] + sign_value * spec_imag
        spec_real = joined_real * cos_turn + joined_imag * sin_turn
        spec_imag = joined_imag * cos_turn - joined_real * sin_turn
    return (spec_real, spec_imag)


def butterfly_inverse(spec_real, spec_imag):
    parts_count = lax.axis_size("ctx")
    device = lax.axis_index("ctx")
    bit_count = parts_count.bit_length() - 1
    for bit_place in range(bit_count):
        sign_value, cos_turn, sin_turn = section_terms(device, bit_place)
        turned_real = spec_real * cos_turn - spec_imag * sin_turn
        turned_imag = spec_imag * cos_turn + spec_real * sin_turn
        partner = pair_swap_back(jnp.stack([turned_real, turned_imag]), bit_place)
        spec_real = 0.5 * (partner[0] + sign_value * turned_real)
        spec_imag = 0.5 * (partner[1] + sign_value * turned_imag)
    angle_value = math.pi * device.astype(jnp.float32) / parts_count
    cos_last = jnp.cos(angle_value)
    sin_last = jnp.sin(angle_value)
    out_real = 0.5 * (spec_real[0] + spec_real[1] * cos_last - spec_imag[1] * sin_last)
    out_imag = 0.5 * (spec_imag[0] + spec_imag[1] * cos_last + spec_real[1] * sin_last)
    return (out_real, out_imag)


def per_device(features, short_weight, long_filter, skip_bias, cotangent):
    taps = short_weight.shape[0]
    token_rows = features[0]
    tokens = token_rows.shape[0]
    channels = long_filter.shape[1]
    parts_count = lax.axis_size("ctx")
    device = lax.axis_index("ctx")
    history = shifted(token_rows[tokens - (taps - 1) :], "ctx", 1)
    extended = jnp.concatenate([history, token_rows], axis=0).astype(jnp.float32)
    mixed_feats = jnp.zeros((tokens, token_rows.shape[1]), jnp.float32)
    for tap_index in range(taps):
        start_row = taps - 1 - tap_index
        mixed_feats = (
            mixed_feats + short_weight[tap_index] * extended[start_row : start_row + tokens]
        )
    query = mixed_feats[:, :channels]
    key_part = mixed_feats[:, channels : 2 * channels]
    value_part = mixed_feats[:, 2 * channels :]
    gated = key_part * value_part
    upstream = cotangent[0].astype(jnp.float32)
    dconv = upstream * query
    signals = jnp.concatenate([gated, long_filter, dconv], axis=1)
    table = spectral_table(device, parts_count, tokens)
    spec_real, spec_imag = butterfly_forward(signals)
    spec_real, spec_imag = local_forward(spec_real, spec_imag, table)
    gated_real = spec_real[..., :channels]
    gated_imag = spec_imag[..., :channels]
    filter_real = spec_real[..., channels : 2 * channels]
    filter_imag = spec_imag[..., channels : 2 * channels]
    dconv_real = spec_real[..., 2 * channels :]
    dconv_imag = spec_imag[..., 2 * channels :]
    conv_real = gated_real * filter_real - gated_imag * filter_imag
    conv_imag = gated_real * filter_imag + gated_imag * filter_real
    back_real = filter_real * dconv_real + filter_imag * dconv_imag
    back_imag = filter_real * dconv_imag - filter_imag * dconv_real
    corr_real = gated_real * dconv_real + gated_imag * dconv_imag
    corr_imag = gated_real * dconv_imag - gated_imag * dconv_real
    inverse_real = jnp.concatenate([conv_real - back_imag, corr_real], axis=-1)
    inverse_imag = jnp.concatenate([conv_imag + back_real, corr_imag], axis=-1)
    inverse_real, inverse_imag = local_inverse(inverse_real, inverse_imag, table)
    result_real, result_imag = butterfly_inverse(inverse_real, inverse_imag)
    long_conv = result_real[:, :channels] + skip_bias * gated
    dgated = result_imag[:, :channels] + skip_bias * dconv
    filter_part = result_real[:, channels:]
    layer_out = (query * long_conv).astype(jnp.bfloat16)[None]
    dmixed = jnp.concatenate([upstream * long_conv, dgated * value_part, dgated * key_part], axis=1)
    later = shifted(dmixed[: taps - 1], "ctx", -1)
    ahead = jnp.concatenate([dmixed, later], axis=0)
    grad_local = jnp.zeros_like(dmixed)
    short_rows = []
    for tap_index in range(taps):
        grad_local = grad_local + short_weight[tap_index] * ahead[tap_index : tap_index + tokens]
        start_row = taps - 1 - tap_index
        short_rows.append(jnp.sum(dmixed * extended[start_row : start_row + tokens], axis=0))
    grad_features = grad_local.astype(jnp.bfloat16)[None]
    short_part = jnp.stack(short_rows)
    skip_part = jnp.sum(dconv * gated, axis=0)
    scale = 1.0 / math.sqrt(lax.axis_size("dp") * parts_count * tokens)
    filter_sum = lax.psum(filter_part, "dp")
    short_sum, skip_sum = lax.psum((short_part, skip_part), ("dp", "ctx"))
    return (layer_out, grad_features, short_sum * scale, filter_sum * scale, skip_sum * scale)


def solution(mesh):
    return jax.shard_map(
        per_device,
        mesh=mesh,
        in_specs=(P("dp", "ctx", None), P(), P("ctx", None), P(), P("dp", "ctx", None)),
        out_specs=(P("dp", "ctx", None), P("dp", "ctx", None), P(), P("ctx", None), P()),
        check_vma=False,
    )
```

profile of v0, /device:TPU:2, one launch (start us, length us, event | category | flops | bytes accessed | tf_op | source)
XLA Modules:
  0.0 1050.0 jit_solution(7923902592177502704)
XLA Ops:
  7.2 0.7 slice_bitcast_fusion.20
  8.0 3.8 collective-permute-start
  11.8 1.3 slice_reduce_fusion.6
  13.2 4.3 collective-permute-done
  17.5 1.1 maximum_convert_fusion
  18.6 0.6 multiply_add_fusion.10
  19.6 1.0 copy-done.15
  21.3 0.5 copy-done.11
  22.0 1.9 pad_maximum_fusion
  23.9 2.4 collective-permute-start.1
  26.5 68.2 %collective-permute-done.1 = f32[2,2,128,1536]{3,2,1,0:T(8,128)} collective-permute-done((f32[2,2,128,1536]{3,2,1,0:T(8,128)}, f32[2,2,128,1536]{3,2,1,0:T(8,128)}, u32[]{:S(2)}, u32[]{:S(2)}) %collective-permute-start.1) | collective-permute-done | bytes 3145760 | tf_op jit(solution)/shard_map/ppermute | solution.py:13
  94.7 3.0 multiply_subtract_fusion.4
  97.7 2.0 pad_maximum_fusion.1
  100.3 67.9 %collective-permute-done.2 = f32[2,2,128,1536]{3,2,1,0:T(8,128)} collective-permute-done((f32[2,2,128,1536]{3,2,1,0:T(8,128)}, f32[2,2,128,1536]{3,2,1,0:T(8,128)}, u32[]{:S(2)}, u32[]{:S(2)}) %collective-permute-start.2) | collective-permute-done | bytes 3145760 | tf_op jit(solution)/shard_map/ppermute | solution.py:13
  168.2 3.1 multiply_subtract_fusion.3
  171.3 2.1 pad_maximum_fusion.2
  174.0 4.0 collective-permute-start.3
  178.1 135.4 %collective-permute-done.3 = f32[2,2,128,1536]{3,2,1,0:T(8,128)} collective-permute-done((f32[2,2,128,1536]{3,2,1,0:T(8,128)}, f32[2,2,128,1536]{3,2,1,0:T(8,128)}, u32[]{:S(2)}, u32[]{:S(2)}) %collective-permute-start.3) | collective-permute-done | bytes 3145760 | tf_op jit(solution)/shard_map/ppermute | solution.py:13
  313.5 3.6 multiply_subtract_fusion.2
  317.1 2.1 pad_maximum_fusion.3
  319.4 137.3 %collective-permute-done.4 = f32[2,2,128,1536]{3,2,1,0:T(8,128)} collective-permute-done((f32[2,2,128,1536]{3,2,1,0:T(8,128)}, f32[2,2,128,1536]{3,2,1,0:T(8,128)}, u32[]{:S(2)}, u32[]{:S(2)}) %collective-permute-start.4) | collective-permute-done | bytes 3145760 | tf_op jit(solution)/shard_map/ppermute | solution.py:13
  456.7 3.1 multiply_add_fusion.1
  459.8 2.0 pad_maximum_fusion.4
  461.9 0.6 copy-done.5
  462.6 69.4 %collective-permute-done.5 = f32[2,2,128,1536]{3,2,1,0:T(8,128)} collective-permute-done((f32[2,2,128,1536]{3,2,1,0:T(8,128)}, f32[2,2,128,1536]{3,2,1,0:T(8,128)}, u32[]{:S(2)}, u32[]{:S(2)}) %collective-permute-start.5) | collective-permute-done | bytes 3145760 | tf_op jit(solution)/shard_map/ppermute | solution.py:13
  532.0 3.5 fusion.2
  535.5 2.0 fusion.32
  537.5 2.0 fusion.33
  539.4 2.0 convolution_add_fusion
  541.4 2.0 convolution_subtract_fusion
  544.0 1.5 fusion.24
  545.6 1.7 fusion.23
  547.3 1.5 convolution_add_fusion.1
  548.8 1.5 convolution_subtract_fusion.1
  550.6 1.5 pad_maximum_fusion.5
  552.4 45.8 %collective-permute-done.6 = f32[2,2,128,1024]{3,2,1,0:T(8,128)} collective-permute-done((f32[2,2,128,1024]{3,2,1,0:T(8,128)}, f32[2,2,128,1024]{3,2,1,0:T(8,128)}, u32[]{:S(2)}, u32[]{:S(2)}) %collective-permute-start.6) | collective-permute-done | bytes 2097184 | tf_op jit(solution)/shard_map/ppermute | solution.py:13
  598.2 2.0 multiply_add_fusion.8
  600.5 0.8 copy-done.6
  601.2 1.5 pad_maximum_fusion.6
  602.7 2.1 collective-permute-start.7
  604.8 89.6 %collective-permute-done.7 = f32[2,2,128,1024]{3,2,1,0:T(8,128)} collective-permute-done((f32[2,2,128,1024]{3,2,1,0:T(8,128)}, f32[2,2,128,1024]{3,2,1,0:T(8,128)}, u32[]{:S(2)}, u32[]{:S(2)}) %collective-permute-start.7) | collective-permute-done | bytes 2097184 | tf_op jit(solution)/shard_map/ppermute | solution.py:13
  694.5 2.3 multiply_add_fusion.7
  697.0 0.8 copy-done.7
  698.1 3.7 collective-permute-start.8
  701.8 92.3 %collective-permute-done.8 = f32[2,2,128,1024]{3,2,1,0:T(8,128)} collective-permute-done((f32[2,2,128,1024]{3,2,1,0:T(8,128)S(1)}, f32[2,2,128,1024]{3,2,1,0:T(8,128)}, u32[]{:S(2)}, u32[]{:S(2)}) %collective-permute-start.8) | collective-permute-done | bytes 2097184 | tf_op jit(solution)/shard_map/ppermute | solution.py:13
  794.1 2.7 multiply_add_fusion.6
  796.8 1.5 pad_maximum_fusion.8
  798.3 0.9 collective-permute-start.9
  799.2 46.3 %collective-permute-done.9 = f32[2,2,128,1024]{3,2,1,0:T(8,128)} collective-permute-done((f32[2,2,128,1024]{3,2,1,0:T(8,128)}, f32[2,2,128,1024]{3,2,1,0:T(8,128)}, u32[]{:S(2)}, u32[]{:S(2)}) %collective-permute-start.9) | collective-permute-done | bytes 2097184 | tf_op jit(solution)/shard_map/ppermute | solution.py:13
  845.5 2.0 multiply_subtract_fusion.5
  847.8 3.2 collective-permute-start.10
  851.0 45.0 %collective-permute-done.10 = f32[2,2,128,1024]{3,2,1,0:T(8,128)S(1)} collective-permute-done((f32[2,2,128,1024]{3,2,1,0:T(8,128)S(1)}, f32[2,2,128,1024]{3,2,1,0:T(8,128)S(1)}, u32[]{:S(2)}, u32[]{:S(2)}) %collective-permute-start.10) | collective-permute-done | bytes 2097184 | tf_op jit(solution)/shard_map/ppermute | solution.py:13
  896.0 0.6 fusion.12
  896.9 0.9 copy-done.10
  897.8 1.0 convert_multiply_fusion
  898.8 0.7 multiply_reduce_fusion
  899.7 75.3 %all-reduce.1 = (f32[7,1536]{1,0:T(8,128)S(1)}, f32[512]{0:T(512)S(1)}) all-reduce(f32[7,1536]{1,0:T(8,128)S(1)} %stack.165, f32[512]{0:T(512)S(1)} %get-tuple-element.21), channel_id=1, replica_groups=mesh['dp'=8,'ctx'=32] {'dp','ctx'}, use_global_device_ids=true, to_apply=%region_7.8 | all-reduce | flops 11264 | bytes 90112 | tf_op jit(solution)/shard_map/psum | solution.py:179
  975.1 0.6 broadcast_multiply_fusion.1
  975.7 4.7 collective-permute-start.11
  980.5 0.6 broadcast_multiply_fusion.2
  981.1 1.1 collective-permute-done.11
  982.3 1.4 fusion.41
  983.7 57.8 %all-reduce.4.cloned.1.call-done = f32[128,512]{1,0:T(8,128)} async-done(((f32[128,512]{1,0:T(8,128)}), f32[128,512]{1,0:T(8,128)}) %all-reduce.4.cloned.1.call-update) | async-done | bytes 262160 | tf_op jit(solution)/shard_map/psum | solution.py:178
  1041.4 1.7 broadcast_multiply_fusion
  (62 shorter events, 5.0 us)
Async XLA Ops:
  7.2 1034.3 %all-reduce.4.cloned.1.call-start = ((), (), s32[]{:S(2)}) async-start(), calls=%async_computation | async-start | bytes 524288 | tf_op jit(solution)/shard_map/psum | solution.py:178
  8.0 9.5 collective-permute-start
  18.6 0.9 copy-start.16
  19.5 1.4 copy-start.9
  19.5 1.1 copy-start.15
  19.6 1.3 copy-start.13
  20.9 0.9 copy-start.11
  20.9 1.1 copy-start.12
  23.9 70.8 %collective-permute-start.1 = (f32[2,2,128,1536]{3,2,1,0:T(8,128)}, f32[2,2,128,1536]{3,2,1,0:T(8,128)}, u32[]{:S(2)}, u32[]{:S(2)}) collective-permute-start(f32[2,2,128,1536]{3,2,1,0:T(8,128)} %pad_maximum_fusion), channel_id=1, source_target_pairs={{0,16},{1,17},{2,18},{3,19},{4,20},{5,21},{6,22},{7,23},{8,24},{9,... | collective-permute-start | bytes 9437192 | tf_op jit(solution)/shard_map/ppermute | solution.py:13
  97.7 2.1 copy-start.1
  99.8 68.4 %collective-permute-start.2 = (f32[2,2,128,1536]{3,2,1,0:T(8,128)}, f32[2,2,128,1536]{3,2,1,0:T(8,128)}, u32[]{:S(2)}, u32[]{:S(2)}) collective-permute-start(f32[2,2,128,1536]{3,2,1,0:T(8,128)} %pad_maximum_fusion.1), channel_id=1, source_target_pairs={{0,8},{1,9},{2,10},{3,11},{4,12},{5,13},{6,14},{7,15},{8,0},{9,1},... | collective-permute-start | bytes 9437192 | tf_op jit(solution)/shard_map/ppermute | solution.py:13
  171.3 2.3 copy-start.2
  171.3 2.7 copy-start.3
  174.0 139.6 %collective-permute-start.3 = (f32[2,2,128,1536]{3,2,1,0:T(8,128)}, f32[2,2,128,1536]{3,2,1,0:T(8,128)}, u32[]{:S(2)}, u32[]{:S(2)}) collective-permute-start(f32[2,2,128,1536]{3,2,1,0:T(8,128)} %pad_maximum_fusion.2), channel_id=1, source_target_pairs={{0,4},{1,5},{2,6},{3,7},{4,0},{5,1},{6,2},{7,3},{8,12},{9,13},{10,... | collective-permute-start | bytes 9437192 | tf_op jit(solution)/shard_map/ppermute | solution.py:13
  317.1 2.1 copy-start
  319.3 137.4 %collective-permute-start.4 = (f32[2,2,128,1536]{3,2,1,0:T(8,128)}, f32[2,2,128,1536]{3,2,1,0:T(8,128)}, u32[]{:S(2)}, u32[]{:S(2)}) collective-permute-start(f32[2,2,128,1536]{3,2,1,0:T(8,128)} %pad_maximum_fusion.3), channel_id=1, source_target_pairs={{0,2},{1,3},{2,0},{3,1},{4,6},{5,7},{6,4},{7,5},{8,10},{9,11},{10,... | collective-permute-start | bytes 9437192 | tf_op jit(solution)/shard_map/ppermute | solution.py:13
  459.8 2.1 copy-start.4
  459.8 2.7 copy-start.5
  462.5 69.5 %collective-permute-start.5 = (f32[2,2,128,1536]{3,2,1,0:T(8,128)}, f32[2,2,128,1536]{3,2,1,0:T(8,128)}, u32[]{:S(2)}, u32[]{:S(2)}) collective-permute-start(f32[2,2,128,1536]{3,2,1,0:T(8,128)} %pad_maximum_fusion.4), channel_id=1, source_target_pairs={{0,1},{1,0},{2,3},{3,2},{4,5},{5,4},{6,7},{7,6},{8,9},{9,8},{10,11... | collective-permute-start | bytes 9437192 | tf_op jit(solution)/shard_map/ppermute | solution.py:13
  552.1 46.1 %collective-permute-start.6 = (f32[2,2,128,1024]{3,2,1,0:T(8,128)}, f32[2,2,128,1024]{3,2,1,0:T(8,128)}, u32[]{:S(2)}, u32[]{:S(2)}) collective-permute-start(f32[2,2,128,1024]{3,2,1,0:T(8,128)} %pad_maximum_fusion.5), channel_id=1, source_target_pairs={{0,1},{1,0},{2,3},{3,2},{4,5},{5,4},{6,7},{7,6},{8,9},{9,8},{10,11... | collective-permute-start | bytes 6291464 | tf_op jit(solution)/shard_map/ppermute | solution.py:13
  600.3 1.0 copy-start.6
  602.7 91.7 %collective-permute-start.7 = (f32[2,2,128,1024]{3,2,1,0:T(8,128)}, f32[2,2,128,1024]{3,2,1,0:T(8,128)}, u32[]{:S(2)}, u32[]{:S(2)}) collective-permute-start(f32[2,2,128,1024]{3,2,1,0:T(8,128)} %pad_maximum_fusion.6), channel_id=1, source_target_pairs={{0,2},{1,3},{2,0},{3,1},{4,6},{5,7},{6,4},{7,5},{8,10},{9,11},{10,... | collective-permute-start | bytes 6291464 | tf_op jit(solution)/shard_map/ppermute | solution.py:13
  696.8 1.0 copy-start.7
  696.8 1.3 copy-start.8
  698.1 96.0 %collective-permute-start.8 = (f32[2,2,128,1024]{3,2,1,0:T(8,128)S(1)}, f32[2,2,128,1024]{3,2,1,0:T(8,128)}, u32[]{:S(2)}, u32[]{:S(2)}) collective-permute-start(f32[2,2,128,1024]{3,2,1,0:T(8,128)S(1)} %pad_maximum_fusion.7), channel_id=1, source_target_pairs={{0,4},{1,5},{2,6},{3,7},{4,0},{5,1},{6,2},{7,3},{8,12},{9,13},{10,... | collective-permute-start | bytes 6291464 | tf_op jit(solution)/shard_map/ppermute | solution.py:13
  798.3 47.3 %collective-permute-start.9 = (f32[2,2,128,1024]{3,2,1,0:T(8,128)}, f32[2,2,128,1024]{3,2,1,0:T(8,128)}, u32[]{:S(2)}, u32[]{:S(2)}) collective-permute-start(f32[2,2,128,1024]{3,2,1,0:T(8,128)} %pad_maximum_fusion.8), channel_id=1, source_target_pairs={{0,8},{1,9},{2,10},{3,11},{4,12},{5,13},{6,14},{7,15},{8,0},{9,1},... | collective-permute-start | bytes 6291464 | tf_op jit(solution)/shard_map/ppermute | solution.py:13
  847.8 48.2 %collective-permute-start.10 = (f32[2,2,128,1024]{3,2,1,0:T(8,128)S(1)}, f32[2,2,128,1024]{3,2,1,0:T(8,128)S(1)}, u32[]{:S(2)}, u32[]{:S(2)}) collective-permute-start(f32[2,2,128,1024]{3,2,1,0:T(8,128)S(1)} %pad_maximum_fusion.9), channel_id=1, source_target_pairs={{0,16},{1,17},{2,18},{3,19},{4,20},{5,21},{6,22},{7,23},{8,24},{9,... | collective-permute-start | bytes 6291464 | tf_op jit(solution)/shard_map/ppermute | solution.py:13
  896.6 1.1 copy-start.10
  896.6 1.2 copy-start.14
  896.6 1.2 copy-start.17
  896.7 1.2 copy-start.18
  975.7 6.5 collective-permute-start.11
Sparse Core Ops, SparseCore 0:
  981.2 60.1 all-reduce.3
where the time goes:
time: 1050 us
  waiting for transfers between devices  860 us (82%)
  blocking collectives  75.3 us (7%)
  other arithmetic  50.7 us (5%)
  starting transfers between devices  25.6 us (2%)
  between operations  15.3 us (1%)
  matrix products  14.2 us (1%)
    ppermute x10, waiting for transfers between devices, swapped(): return lax.ppermute(value, axis, pairs)  797 us
    psum x1, blocking collectives, per_device(): short_sum, skip_sum = lax.psum((short_part, skip_part), ('dp', 'ctx'))  75.3 us
    psum x1, waiting for transfers between devices, per_device(): filter_sum = lax.psum(filter_part, 'dp')  57.8 us
  transfers between devices with their start and end apart: 13, of which 13 were waited for; matrix products, arithmetic and copies ran while one was open for 0% of the time, Pallas kernels for 0%

commit v1 on v0

--- a/solution.py
+++ b/solution.py
@@ -175,7 +175,10 @@
     short_part = jnp.stack(short_rows)
     skip_part = jnp.sum(dconv * gated, axis=0)
     scale = 1.0 / math.sqrt(lax.axis_size("dp") * parts_count * tokens)
-    filter_sum = lax.psum(filter_part, "dp")
+    size, filter_sum = (lax.axis_size("dp"), filter_part)
+    for stride in [1 << k for k in range(size.bit_length() - 1)]:
+        pairs_2 = [(i, i ^ stride) for i in range(size)]
+        filter_sum = filter_sum + lax.ppermute(filter_sum, "dp", pairs_2)
     short_sum, skip_sum = lax.psum((short_part, skip_part), ("dp", "ctx"))
     return (layer_out, grad_features, short_sum * scale, filter_sum * scale, skip_sum * scale)
 

time: 1050 us -> 989 us (0.942)
  waiting for transfers between devices: 860 us -> 810 us
  between operations: 15.3 us -> 1.95 us
    psum x1 -> x0, waiting for transfers between devices: 57.8 us -> none  [per_device(): filter_sum = lax.psum(filter_part, 'dp')]
  transfers between devices with their start and end apart: 13 -> 15, of which waited for: 13 -> 14; matrix products, arithmetic and copies ran while one was open for 0% -> 0% of each run, Pallas kernels for 0% -> 0%
where the time goes in v1:
time: 989 us; the launch traced here: 988 us
  waiting for transfers between devices  810 us (82%)
  blocking collectives  75.2 us (8%)
  other arithmetic  50 us (5%)
  starting transfers between devices  29.3 us (3%)
  matrix products  14.2 us (1%)
    ppermute x10, waiting for transfers between devices, swapped(): return lax.ppermute(value, axis, pairs)  797 us
    psum x1, blocking collectives, per_device(): short_sum, skip_sum = lax.psum((short_part, skip_part), ('dp', 'ctx'))  75.2 us
  transfers between devices with their start and end apart: 15, of which 14 were waited for; matrix products, arithmetic and copies ran while one was open for 0% of the time, Pallas kernels for 0%

profile of v1, /device:TPU:2, one launch (start us, length us, event | category | flops | bytes accessed | tf_op | source)
XLA Modules:
  0.0 987.9 jit_solution(6441329548320270847)
XLA Ops:
  0.6 0.7 slice_bitcast_fusion.20
  1.4 3.8 collective-permute-start
  5.2 1.3 slice_reduce_fusion.6
  6.7 4.3 collective-permute-done
  10.9 1.1 maximum_convert_fusion
  12.0 0.6 multiply_add_fusion.10
  13.0 1.0 copy-done.15
  15.4 1.9 pad_maximum_fusion
  17.3 2.4 collective-permute-start.1
  19.9 68.2 %collective-permute-done.1 = f32[2,2,128,1536]{3,2,1,0:T(8,128)} collective-permute-done((f32[2,2,128,1536]{3,2,1,0:T(8,128)}, f32[2,2,128,1536]{3,2,1,0:T(8,128)}, u32[]{:S(2)}, u32[]{:S(2)}) %collective-permute-start.1) | collective-permute-done | bytes 3145760 | tf_op jit(solution)/shard_map/ppermute | solution.py:13
  88.1 3.0 multiply_subtract_fusion.4
  91.2 2.0 pad_maximum_fusion.1
  93.7 67.9 %collective-permute-done.2 = f32[2,2,128,1536]{3,2,1,0:T(8,128)} collective-permute-done((f32[2,2,128,1536]{3,2,1,0:T(8,128)}, f32[2,2,128,1536]{3,2,1,0:T(8,128)}, u32[]{:S(2)}, u32[]{:S(2)}) %collective-permute-start.2) | collective-permute-done | bytes 3145760 | tf_op jit(solution)/shard_map/ppermute | solution.py:13
  161.6 3.1 multiply_subtract_fusion.3
  164.7 2.1 pad_maximum_fusion.2
  167.4 4.0 collective-permute-start.3
  171.6 135.3 %collective-permute-done.3 = f32[2,2,128,1536]{3,2,1,0:T(8,128)} collective-permute-done((f32[2,2,128,1536]{3,2,1,0:T(8,128)}, f32[2,2,128,1536]{3,2,1,0:T(8,128)}, u32[]{:S(2)}, u32[]{:S(2)}) %collective-permute-start.3) | collective-permute-done | bytes 3145760 | tf_op jit(solution)/shard_map/ppermute | solution.py:13
  306.9 3.6 multiply_subtract_fusion.2
  310.6 2.1 pad_maximum_fusion.3
  312.9 137.3 %collective-permute-done.4 = f32[2,2,128,1536]{3,2,1,0:T(8,128)} collective-permute-done((f32[2,2,128,1536]{3,2,1,0:T(8,128)}, f32[2,2,128,1536]{3,2,1,0:T(8,128)}, u32[]{:S(2)}, u32[]{:S(2)}) %collective-permute-start.4) | collective-permute-done | bytes 3145760 | tf_op jit(solution)/shard_map/ppermute | solution.py:13
  450.1 3.1 multiply_add_fusion.1
  453.2 2.0 pad_maximum_fusion.4
  455.3 0.6 copy-done.5
  456.0 69.4 %collective-permute-done.5 = f32[2,2,128,1536]{3,2,1,0:T(8,128)} collective-permute-done((f32[2,2,128,1536]{3,2,1,0:T(8,128)}, f32[2,2,128,1536]{3,2,1,0:T(8,128)}, u32[]{:S(2)}, u32[]{:S(2)}) %collective-permute-start.5) | collective-permute-done | bytes 3145760 | tf_op jit(solution)/shard_map/ppermute | solution.py:13
  525.4 3.5 fusion.2
  528.9 2.0 fusion.32
  530.9 2.0 fusion.33
  532.9 2.0 convolution_add_fusion
  534.8 2.0 convolution_subtract_fusion
  537.5 1.5 fusion.24
  539.0 1.7 fusion.23
  540.7 1.5 convolution_add_fusion.1
  542.2 1.5 convolution_subtract_fusion.1
  544.0 1.5 pad_maximum_fusion.5
  545.8 45.8 %collective-permute-done.6 = f32[2,2,128,1024]{3,2,1,0:T(8,128)} collective-permute-done((f32[2,2,128,1024]{3,2,1,0:T(8,128)}, f32[2,2,128,1024]{3,2,1,0:T(8,128)}, u32[]{:S(2)}, u32[]{:S(2)}) %collective-permute-start.6) | collective-permute-done | bytes 2097184 | tf_op jit(solution)/shard_map/ppermute | solution.py:13
  591.6 2.0 multiply_add_fusion.8
  593.8 0.8 copy-done.6
  594.6 1.5 pad_maximum_fusion.6
  596.1 2.2 collective-permute-start.7
  598.3 89.6 %collective-permute-done.7 = f32[2,2,128,1024]{3,2,1,0:T(8,128)} collective-permute-done((f32[2,2,128,1024]{3,2,1,0:T(8,128)}, f32[2,2,128,1024]{3,2,1,0:T(8,128)}, u32[]{:S(2)}, u32[]{:S(2)}) %collective-permute-start.7) | collective-permute-done | bytes 2097184 | tf_op jit(solution)/shard_map/ppermute | solution.py:13
  687.9 2.3 multiply_add_fusion.7
  690.4 0.8 copy-done.7
  691.6 3.8 collective-permute-start.8
  695.4 92.3 %collective-permute-done.8 = f32[2,2,128,1024]{3,2,1,0:T(8,128)} collective-permute-done((f32[2,2,128,1024]{3,2,1,0:T(8,128)S(1)}, f32[2,2,128,1024]{3,2,1,0:T(8,128)}, u32[]{:S(2)}, u32[]{:S(2)}) %collective-permute-start.8) | collective-permute-done | bytes 2097184 | tf_op jit(solution)/shard_map/ppermute | solution.py:13
  787.7 2.7 multiply_add_fusion.6
  790.3 1.5 pad_maximum_fusion.8
  791.8 0.9 collective-permute-start.9
  792.7 46.2 %collective-permute-done.9 = f32[2,2,128,1024]{3,2,1,0:T(8,128)} collective-permute-done((f32[2,2,128,1024]{3,2,1,0:T(8,128)}, f32[2,2,128,1024]{3,2,1,0:T(8,128)}, u32[]{:S(2)}, u32[]{:S(2)}) %collective-permute-start.9) | collective-permute-done | bytes 2097184 | tf_op jit(solution)/shard_map/ppermute | solution.py:13
  839.0 2.0 multiply_subtract_fusion.5
  841.2 3.3 collective-permute-start.10
  844.5 45.0 %collective-permute-done.10 = f32[2,2,128,1024]{3,2,1,0:T(8,128)S(1)} collective-permute-done((f32[2,2,128,1024]{3,2,1,0:T(8,128)S(1)}, f32[2,2,128,1024]{3,2,1,0:T(8,128)S(1)}, u32[]{:S(2)}, u32[]{:S(2)}) %collective-permute-start.10) | collective-permute-done | bytes 2097184 | tf_op jit(solution)/shard_map/ppermute | solution.py:13
  889.5 0.6 fusion.12
  890.6 1.5 collective-permute-done.12
  892.1 0.9 convert_multiply_fusion
  893.0 1.6 collective-permute-start.13
  894.6 0.7 multiply_reduce_fusion
  895.5 75.2 %all-reduce.1 = (f32[7,1536]{1,0:T(8,128)S(1)}, f32[512]{0:T(512)S(1)}) all-reduce(f32[7,1536]{1,0:T(8,128)S(1)} %stack.165, f32[512]{0:T(512)S(1)} %get-tuple-element.21), channel_id=1, replica_groups=mesh['dp'=8,'ctx'=32] {'dp','ctx'}, use_global_device_ids=true, to_apply=%region_7.8 | all-reduce | flops 11264 | bytes 90112 | tf_op jit(solution)/shard_map/psum | solution.py:182
  970.8 0.6 broadcast_multiply_fusion
  971.4 5.1 collective-permute-start.11
  977.1 1.1 collective-permute-done.11
  978.4 1.5 collective-permute-start.14
  979.9 1.4 fusion.41
  981.3 5.9 collective-permute-done.14
  987.2 0.7 add_multiply_fusion
  (67 shorter events, 6.0 us)
Async XLA Ops:
  1.4 9.5 collective-permute-start
  12.0 0.9 copy-start.16
  12.9 1.4 copy-start.9
  12.9 1.1 copy-start.15
  13.0 1.3 copy-start.13
  14.3 0.9 copy-start.11
  14.3 1.1 copy-start.12
  17.3 70.8 %collective-permute-start.1 = (f32[2,2,128,1536]{3,2,1,0:T(8,128)}, f32[2,2,128,1536]{3,2,1,0:T(8,128)}, u32[]{:S(2)}, u32[]{:S(2)}) collective-permute-start(f32[2,2,128,1536]{3,2,1,0:T(8,128)} %pad_maximum_fusion), channel_id=1, source_target_pairs={{0,16},{1,17},{2,18},{3,19},{4,20},{5,21},{6,22},{7,23},{8,24},{9,... | collective-permute-start | bytes 9437192 | tf_op jit(solution)/shard_map/ppermute | solution.py:13
  91.1 2.1 copy-start.1
  93.3 68.4 %collective-permute-start.2 = (f32[2,2,128,1536]{3,2,1,0:T(8,128)}, f32[2,2,128,1536]{3,2,1,0:T(8,128)}, u32[]{:S(2)}, u32[]{:S(2)}) collective-permute-start(f32[2,2,128,1536]{3,2,1,0:T(8,128)} %pad_maximum_fusion.1), channel_id=1, source_target_pairs={{0,8},{1,9},{2,10},{3,11},{4,12},{5,13},{6,14},{7,15},{8,0},{9,1},... | collective-permute-start | bytes 9437192 | tf_op jit(solution)/shard_map/ppermute | solution.py:13
  164.7 2.3 copy-start.2
  164.7 2.7 copy-start.3
  167.4 139.5 %collective-permute-start.3 = (f32[2,2,128,1536]{3,2,1,0:T(8,128)}, f32[2,2,128,1536]{3,2,1,0:T(8,128)}, u32[]{:S(2)}, u32[]{:S(2)}) collective-permute-start(f32[2,2,128,1536]{3,2,1,0:T(8,128)} %pad_maximum_fusion.2), channel_id=1, source_target_pairs={{0,4},{1,5},{2,6},{3,7},{4,0},{5,1},{6,2},{7,3},{8,12},{9,13},{10,... | collective-permute-start | bytes 9437192 | tf_op jit(solution)/shard_map/ppermute | solution.py:13
  310.6 2.1 copy-start
  312.7 137.4 %collective-permute-start.4 = (f32[2,2,128,1536]{3,2,1,0:T(8,128)}, f32[2,2,128,1536]{3,2,1,0:T(8,128)}, u32[]{:S(2)}, u32[]{:S(2)}) collective-permute-start(f32[2,2,128,1536]{3,2,1,0:T(8,128)} %pad_maximum_fusion.3), channel_id=1, source_target_pairs={{0,2},{1,3},{2,0},{3,1},{4,6},{5,7},{6,4},{7,5},{8,10},{9,11},{10,... | collective-permute-start | bytes 9437192 | tf_op jit(solution)/shard_map/ppermute | solution.py:13
  453.2 2.1 copy-start.4
  453.2 2.7 copy-start.5
  455.9 69.5 %collective-permute-start.5 = (f32[2,2,128,1536]{3,2,1,0:T(8,128)}, f32[2,2,128,1536]{3,2,1,0:T(8,128)}, u32[]{:S(2)}, u32[]{:S(2)}) collective-permute-start(f32[2,2,128,1536]{3,2,1,0:T(8,128)} %pad_maximum_fusion.4), channel_id=1, source_target_pairs={{0,1},{1,0},{2,3},{3,2},{4,5},{5,4},{6,7},{7,6},{8,9},{9,8},{10,11... | collective-permute-start | bytes 9437192 | tf_op jit(solution)/shard_map/ppermute | solution.py:13
  545.5 46.1 %collective-permute-start.6 = (f32[2,2,128,1024]{3,2,1,0:T(8,128)}, f32[2,2,128,1024]{3,2,1,0:T(8,128)}, u32[]{:S(2)}, u32[]{:S(2)}) collective-permute-start(f32[2,2,128,1024]{3,2,1,0:T(8,128)} %pad_maximum_fusion.5), channel_id=1, source_target_pairs={{0,1},{1,0},{2,3},{3,2},{4,5},{5,4},{6,7},{7,6},{8,9},{9,8},{10,11... | collective-permute-start | bytes 6291464 | tf_op jit(solution)/shard_map/ppermute | solution.py:13
  593.6 1.0 copy-start.6
  596.1 91.8 %collective-permute-start.7 = (f32[2,2,128,1024]{3,2,1,0:T(8,128)}, f32[2,2,128,1024]{3,2,1,0:T(8,128)}, u32[]{:S(2)}, u32[]{:S(2)}) collective-permute-start(f32[2,2,128,1024]{3,2,1,0:T(8,128)} %pad_maximum_fusion.6), channel_id=1, source_target_pairs={{0,2},{1,3},{2,0},{3,1},{4,6},{5,7},{6,4},{7,5},{8,10},{9,11},{10,... | collective-permute-start | bytes 6291464 | tf_op jit(solution)/shard_map/ppermute | solution.py:13
  690.2 1.0 copy-start.7
  690.2 1.3 copy-start.8
  691.6 96.1 %collective-permute-start.8 = (f32[2,2,128,1024]{3,2,1,0:T(8,128)S(1)}, f32[2,2,128,1024]{3,2,1,0:T(8,128)}, u32[]{:S(2)}, u32[]{:S(2)}) collective-permute-start(f32[2,2,128,1024]{3,2,1,0:T(8,128)S(1)} %pad_maximum_fusion.7), channel_id=1, source_target_pairs={{0,4},{1,5},{2,6},{3,7},{4,0},{5,1},{6,2},{7,3},{8,12},{9,13},{10,... | collective-permute-start | bytes 6291464 | tf_op jit(solution)/shard_map/ppermute | solution.py:13
  791.8 47.1 %collective-permute-start.9 = (f32[2,2,128,1024]{3,2,1,0:T(8,128)}, f32[2,2,128,1024]{3,2,1,0:T(8,128)}, u32[]{:S(2)}, u32[]{:S(2)}) collective-permute-start(f32[2,2,128,1024]{3,2,1,0:T(8,128)} %pad_maximum_fusion.8), channel_id=1, source_target_pairs={{0,8},{1,9},{2,10},{3,11},{4,12},{5,13},{6,14},{7,15},{8,0},{9,1},... | collective-permute-start | bytes 6291464 | tf_op jit(solution)/shard_map/ppermute | solution.py:13
  841.2 48.3 %collective-permute-start.10 = (f32[2,2,128,1024]{3,2,1,0:T(8,128)S(1)}, f32[2,2,128,1024]{3,2,1,0:T(8,128)S(1)}, u32[]{:S(2)}, u32[]{:S(2)}) collective-permute-start(f32[2,2,128,1024]{3,2,1,0:T(8,128)S(1)} %pad_maximum_fusion.9), channel_id=1, source_target_pairs={{0,16},{1,17},{2,18},{3,19},{4,20},{5,21},{6,22},{7,23},{8,24},{9,... | collective-permute-start | bytes 6291464 | tf_op jit(solution)/shard_map/ppermute | solution.py:13
  890.2 1.9 copy-start.10
  890.2 1.9 copy-start.14
  890.2 1.9 copy-start.17
  890.2 1.9 copy-start.18
  890.5 1.6 collective-permute-start.12
  893.0 85.3 %collective-permute-start.13 = (f32[128,512]{1,0:T(8,128)S(1)}, f32[128,512]{1,0:T(8,128)S(1)}, u32[]{:S(2)}, u32[]{:S(2)}) collective-permute-start(f32[128,512]{1,0:T(8,128)S(1)} %get-tuple-element.64), channel_id=1, source_target_pairs={{0,64},{32,96},{64,0},{96,32},{128,192},{160,224},{192,128},{224,1... | collective-permute-start | bytes 786440 | tf_op jit(solution)/shard_map/ppermute | solution.py:181
  971.4 6.9 collective-permute-start.11
  978.4 8.8 collective-permute-start.14
